TPU v7x, 32 devices: a whole 2x2x4 slice. The times are simulated.
32 devices in a mesh: groups: 2 (over x), seq: 16 (over z, y, core).
Axes of the slice: x: 2, y: 2, z: 4, core: 2. Of those that a mesh axis runs over, the one named last changes fastest.
Arguments:
- hidden: bfloat16 [4096, 8192], P(('groups', 'seq')), parts along dimension 0, may hold values from -6 to 6
- q_base: bfloat16 [4096, 8192], P(('groups', 'seq')), parts along dimension 0, may hold values from -8 to 8
- base_key_weight: bfloat16 [4096, 1024], P(('groups', 'seq')), parts along dimension 0, may hold values from -8 to 8
- base_value_weight: bfloat16 [4096, 1024], P(('groups', 'seq')), parts along dimension 0, may hold values from -6 to 6
- shrink_a: bfloat16 [32, 8192, 192], P('groups', 'seq'), parts along dimension 0, may hold values from -0.0625 to 0.0625
- expand_q: bfloat16 [32, 64, 8192], P('groups', None, 'seq'), parts along dimension 0, may hold values from -0.375 to 0.375
- key_value_up_weight: bfloat16 [32, 64, 2048], P('groups'), parts along dimension 0, may hold values from -0.375 to 0.375
- block_request: int32 [64], P('groups'), parts along dimension 0, may hold values from 0 to 7, never falling along the last dimension, each value on 1 to 16 neighbouring positions
- request_adapter: int32 [16], P('groups'), parts along dimension 0, may hold values from 0 to 15
Outputs:
- attended: bfloat16 [4096, 8192], P(('groups', 'seq')), parts along dimension 0
There are 2 independent parts, one for each index of `groups`. A program takes and returns all parts, laid end to end along the dimension named above; each array names one. Nothing has to cross between parts.
Inputs may be any that keep to these rules, and one draw needn't show every extreme that they name: `block_request`: each request holds 1 to 16 consecutive blocks, request numbers never fall along the blocks, and some request holds exactly 16 blocks.
All inputs are finite; a program needn't handle non-finite values.
Results may differ from a plain program's by a relative error of at most 0.012.
The roundings to bfloat16 on the way count: a program that leaves them out, or rounds other values in their place, can miss the bound.
Values may be sent and summed in bfloat16 or wider, within the bound.
No kernel may reach another device: no remote copies, remote signals or barrier semaphores. Data moves between devices by JAX's collectives and lax.ppermute only.
A program may use at most 128 MiB of HBM per device.

v0:
```python
import math
import jax
import jax.numpy as jnp
from jax import lax
from jax.sharding import PartitionSpec as P

QUERY_HEADS = 64
KEY_VALUE_HEADS = 8
HEAD_SIZE = 128
ADAPTER_RANK = 64
QBLK = 512


def body(
    hidden,
    q_base,
    base_key_weight,
    base_value_weight,
    shrink_a,
    expand_q,
    key_value_up_weight,
    block_request,
    request_adapter,
):
    token_per_device = hidden.shape[0]
    device_list = lax.axis_size("seq")
    my_index = lax.axis_index("seq")
    token_total = token_per_device * device_list
    block_count = block_request.shape[0]
    block_len = token_total // block_count
    most_blocks = min(32, block_count // 2)
    key_window = QBLK + most_blocks * block_len
    heads_dev = QUERY_HEADS // device_list
    device_groups = device_list // KEY_VALUE_HEADS
    key_value_head = my_index // device_groups
    request_count = request_adapter.shape[0]
    adapter_number = key_value_up_weight.shape[0]
    slice_width = shrink_a.shape[1]
    picked = block_request[:, None] == jnp.arange(request_count, dtype=jnp.int32)[None, :]
    adapter_of = jnp.sum(jnp.where(picked, request_adapter[None, :], 0), axis=1)
    feature_rows = lax.all_to_all(hidden, "seq", split_axis=1, concat_axis=0, tiled=True)
    partial_value = jnp.einsum(
        "btf,bfr->btr",
        feature_rows.reshape(block_count, block_len, slice_width),
        shrink_a[adapter_of],
        preferred_element_type=jnp.float32,
    ).reshape(token_total, 3 * ADAPTER_RANK)
    shrunk = lax.psum(partial_value, "seq").astype(jnp.bfloat16)
    key_replicas = jnp.repeat(
        base_key_weight.reshape(token_per_device, KEY_VALUE_HEADS, HEAD_SIZE), device_groups, axis=1
    ).reshape(token_per_device, device_list * HEAD_SIZE)
    value_replicas = jnp.repeat(
        base_value_weight.reshape(token_per_device, KEY_VALUE_HEADS, HEAD_SIZE),
        device_groups,
        axis=1,
    ).reshape(token_per_device, device_list * HEAD_SIZE)
    q_heads, k_one, v_one = (
        lax.all_to_all(q_base, "seq", split_axis=1, concat_axis=0, tiled=True),
        lax.all_to_all(key_replicas, "seq", split_axis=1, concat_axis=0, tiled=True),
        lax.all_to_all(value_replicas, "seq", split_axis=1, concat_axis=0, tiled=True),
    )
    low_blocks = shrunk.reshape(block_count, block_len, 3, ADAPTER_RANK)
    q_delta = jnp.einsum(
        "btr,brc->btc",
        low_blocks[:, :, 0],
        expand_q[adapter_of],
        preferred_element_type=jnp.float32,
    ).reshape(token_total, heads_dev * HEAD_SIZE)
    query_rows = (
        (q_heads.astype(jnp.float32) + q_delta)
        .astype(jnp.bfloat16)
        .reshape(token_total, heads_dev, HEAD_SIZE)
    )
    kv_table = lax.dynamic_index_in_dim(
        key_value_up_weight.reshape(adapter_number, ADAPTER_RANK, 2, KEY_VALUE_HEADS, HEAD_SIZE),
        key_value_head,
        axis=3,
        keepdims=False,
    )
    kv_delta = jnp.einsum(
        "btcr,brcd->btcd",
        low_blocks[:, :, 1:],
        kv_table[adapter_of],
        preferred_element_type=jnp.float32,
    ).reshape(token_total, 2, HEAD_SIZE)
    key_rows = (k_one.astype(jnp.float32) + kv_delta[:, 0]).astype(jnp.bfloat16)
    value_rows = (v_one.astype(jnp.float32) + kv_delta[:, 1]).astype(jnp.bfloat16)
    request_of = jnp.repeat(block_request, block_len)
    score_scale = 1.0 / math.sqrt(HEAD_SIZE)

    def attend(block_index):
        q_start = block_index * QBLK
        k_start = jnp.clip(q_start + QBLK - key_window, 0, token_total - key_window)
        q_rows = lax.dynamic_slice_in_dim(query_rows, q_start, QBLK, 0)
        k_rows = lax.dynamic_slice_in_dim(key_rows, k_start, key_window, 0)
        v_rows = lax.dynamic_slice_in_dim(value_rows, k_start, key_window, 0)
        q_request = lax.dynamic_slice_in_dim(request_of, q_start, QBLK, 0)
        k_request = lax.dynamic_slice_in_dim(request_of, k_start, key_window, 0)
        q_pos = q_start + jnp.arange(QBLK, dtype=jnp.int32)
        k_pos = k_start + jnp.arange(key_window, dtype=jnp.int32)
        allowed = (k_pos[None, :] <= q_pos[:, None]) & (k_request[None, :] == q_request[:, None])
        scores = (
            jnp.einsum("qhd,kd->hqk", q_rows, k_rows, preferred_element_type=jnp.float32)
            * score_scale
        )
        scores = jnp.where(allowed[None], scores, -1e30)
        row_max = jnp.max(scores, axis=-1, keepdims=True)
        weights = jnp.exp(scores - row_max)
        probs = (weights / jnp.sum(weights, axis=-1, keepdims=True)).astype(jnp.bfloat16)
        result = jnp.einsum("hqk,kd->qhd", probs, v_rows, preferred_element_type=jnp.float32)
        return result.astype(jnp.bfloat16).reshape(QBLK, heads_dev * HEAD_SIZE)

    blocks_out = lax.map(attend, jnp.arange(token_total // QBLK, dtype=jnp.int32))
    head_rows = blocks_out.reshape(token_total, heads_dev * HEAD_SIZE)
    return lax.all_to_all(head_rows, "seq", split_axis=0, concat_axis=1, tiled=True)


def solution(mesh):
    return jax.shard_map(
        body,
        mesh=mesh,
        in_specs=(
            P(("groups", "seq"), None),
            P(("groups", "seq"), None),
            P(("groups", "seq"), None),
            P(("groups", "seq"), None),
            P("groups", "seq", None),
            P("groups", None, "seq"),
            P("groups", None, None),
            P("groups"),
            P("groups"),
        ),
        out_specs=P(("groups", "seq"), None),
        check_vma=False,
    )
```

profile of v0, /device:TPU:1, one launch (start us, length us, event | category | flops | bytes accessed | tf_op | source)
XLA Modules:
  0.0 373.0 jit_solution(3717521788086597597)
XLA Ops:
  2.0 7.3 %all-to-all-start = ((bf16[128,16,128]{2,0,1:T(8,128)(2,1)}), bf16[128,16,128]{2,0,1:T(8,128)(2,1)}, u32[]{:S(2)}, u32[]{:S(2)}) async-start(bf16[128,16,128]{2,0,1:T(8,128)(2,1)} %bitcast.117), calls=%async_computation | async-start | bytes 1048576 | tf_op jit(solution)/shard_map/all_to_all | solution.py:60
  12.5 11.0 %all-to-all-done = bf16[128,16,128]{2,0,1:T(8,128)(2,1)} async-done(((bf16[128,16,128]{2,0,1:T(8,128)(2,1)}), bf16[128,16,128]{2,0,1:T(8,128)(2,1)}, u32[]{:S(2)}, u32[]{:S(2)}) %all-to-all-start) | async-done | bytes 524320 | tf_op jit(solution)/shard_map/all_to_all | solution.py:60
  23.5 4.5 %all-to-all-start.1 = ((bf16[128,16,512]{2,0,1:T(8,128)(2,1)}), bf16[128,16,512]{2,0,1:T(8,128)(2,1)}, u32[]{:S(2)}, u32[]{:S(2)}) async-start(bf16[128,16,512]{2,0,1:T(8,128)(2,1)} %bitcast.109), calls=%async_computation.1 | async-start | bytes 4194304 | tf_op jit(solution)/shard_map/all_to_all | solution.py:41
  32.1 37.6 %all-to-all-done.1 = bf16[128,16,512]{2,0,1:T(8,128)(2,1)} async-done(((bf16[128,16,512]{2,0,1:T(8,128)(2,1)}), bf16[128,16,512]{2,0,1:T(8,128)(2,1)}, u32[]{:S(2)}, u32[]{:S(2)}) %all-to-all-start.1) | async-done | bytes 2097184 | tf_op jit(solution)/shard_map/all_to_all | solution.py:41
  69.7 10.7 %all-to-all-start.3 = ((bf16[128,16,512]{0,2,1:T(8,128)(2,1)}), bf16[128,16,512]{0,2,1:T(8,128)(2,1)}, u32[]{:S(2)}, u32[]{:S(2)}) async-start(bf16[128,16,512]{0,2,1:T(8,128)(2,1)} %bitcast.107), calls=%async_computation.3 | async-start | bytes 4194304 | tf_op jit(solution)/shard_map/all_to_all | solution.py:58
  80.4 5.6 %copy.89 = bf16[128,8,16,128]{3,2,1,0:T(8,128)(2,1)} copy(bf16[128,8,16,128]{3,1,2,0:T(8,128)(2,1)} %bitcast.114) | data formatting | bytes 8388608
  101.0 5.5 %fusion.26 = f32[32,192,64]{1,2,0:T(8,128)S(1)} fusion(bf16[32,512,192]{1,2,0:T(8,128)(2,1)} %gather_fusion.1, bf16[32,64,512]{2,1,0:T(8,128)(2,1)} %bitcast.13), kind=kOutput, calls=%fused_computation.50 | convolution fusion | flops 402653184 | bytes 9961472 | tf_op jit(solution)/shard_map/btf,bfr->btr/dot_general | solution.py:42
  108.2 70.1 %all-reduce.1 = bf16[2048,192]{0,1:T(8,128)(2,1)S(1)} all-reduce(f32[2048,192]{0,1:T(8,128)} %copy.66), channel_id=1, replica_groups=mesh['groups'=2,'seq'=16] {'seq'}, use_global_device_ids=true, to_apply=%region_1.2 | all-reduce | flops 393216 | bytes 2359296 | tf_op jit(solution)/shard_map/psum | solution.py:48
  187.8 5.3 %reshape.150 = f32[2048,4,128]{2,1,0:T(4,128)} reshape(f32[32,64,512]{2,1,0:T(8,128)} %fusion.22) | data formatting | bytes 8388608 | tf_op jit(solution)/shard_map/reshape | solution.py:68
  193.1 5.3 %copy.73 = f32[2048,4,128]{0,2,1:T(8,128)} copy(f32[2048,4,128]{2,1,0:T(4,128)} %reshape.150) | data formatting | bytes 8388608 | tf_op jit(solution)/shard_map/reshape | solution.py:68
  199.3 8.5 %all-to-all-start.2 = ((bf16[128,16,128]{2,0,1:T(8,128)(2,1)}), bf16[128,16,128]{2,0,1:T(8,128)(2,1)S(1)}, u32[]{:S(2)}, u32[]{:S(2)}) async-start(bf16[128,16,128]{2,0,1:T(8,128)(2,1)} %bitcast.19), calls=%async_computation.2 | async-start | bytes 1048576 | tf_op jit(solution)/shard_map/all_to_all | solution.py:59
  209.8 4.4 %copy.71 = f32[16,128,512]{1,0,2:T(8,128)} copy(f32[16,128,512]{1,2,0:T(8,128)S(1)} %convert_bitcast_fusion) | data formatting | bytes 8388608 | tf_op jit(solution)/shard_map/convert_element_type | solution.py:70
  214.2 4.9 %reshape.153 = f32[2048,4,128]{0,2,1:T(8,128)} reshape(f32[16,128,512]{1,0,2:T(8,128)} %copy.71) | data formatting | bytes 8388608 | tf_op jit(solution)/shard_map/convert_element_type | solution.py:70
  219.1 5.4 %add_convert_fusion = bf16[2048,4,128]{0,2,1:T(8,128)(2,1)} fusion(f32[2048,4,128]{0,2,1:T(8,128)} %reshape.153, f32[2048,4,128]{0,2,1:T(8,128)} %copy.73), kind=kLoop, calls=%fused_computation.28 | loop fusion | flops 2097152 | bytes 10485760 | tf_op jit(solution)/shard_map/convert_element_type | solution.py:71
  226.6 84.4 %while.14 = (s32[]{:T(128)}, bf16[4,512,512]{2,1,0:T(8,128)(2,1)}, s32[4]{0:T(128)S(1)}, bf16[2048,128]{1,0:T(8,128)(2,1)}, s32[2048]{0:T(1024)S(1)}, /*index=5*...) while((s32[]{:T(128)}, bf16[4,512,512]{2,1,0:T(8,128)(2,1)}, ...), condition=%wide.region_5.6_spmd, body=%wide.region_2.5_spmd.sunk | while | flops 1638403584 | bytes 57991952 | solution.py:113
  232.1 8.9 %fusion.43 = (f32[4,512]{1,0:T(4,128)S(1)}, f32[4,512,1536]{1,2,0:T(8,128)}) fusion(f32[1536,512,4]{1,0,2:T(8,128)S(1)} %fusion.42, pred[512,1536]{0,1:T(8,128)(4,1)S(1)} %compare_and_fusion.2), kind=kOutput, calls=%fused_computation.49.clone.1 | output fusion | flops 18875904 | bytes 25960448 | tf_op jit(solution)/shard_map/while/body/eval_jaxpr/sub | solution.py:108
  241.0 5.6 %fusion.44 = bf16[128,4,512]{2,0,1:T(8,128)(2,1)S(1)} fusion(f32[4,512,1536]{1,2,0:T(8,128)} %get-tuple-element.245, f32[4,512]{1,0:T(4,128)S(1)} %get-tuple-element.246, bf16[2048,128]{1,0:T(8,128)(2,1)S(1)} %copy-done.5, s32[]{:T(128)S(6)} %min.11), kind=kOutput, calls=%fused_computation.13.clone.1 | convolution fusion | flops 811859968 | bytes 13508612 | tf_op jit(solution)/shard_map/while/body/eval_jaxpr/hqk,kd->qhd/dot_general | solution.py:110
  253.2 8.9 %fusion.43 = (f32[4,512]{1,0:T(4,128)S(1)}, f32[4,512,1536]{1,2,0:T(8,128)}) fusion(f32[1536,512,4]{1,0,2:T(8,128)S(1)} %fusion.42, pred[512,1536]{0,1:T(8,128)(4,1)S(1)} %compare_and_fusion.2), kind=kOutput, calls=%fused_computation.49.clone.1 | output fusion | flops 18875904 | bytes 25960448 | tf_op jit(solution)/shard_map/while/body/eval_jaxpr/sub | solution.py:108
  262.1 5.6 %fusion.44 = bf16[128,4,512]{2,0,1:T(8,128)(2,1)S(1)} fusion(f32[4,512,1536]{1,2,0:T(8,128)} %get-tuple-element.245, f32[4,512]{1,0:T(4,128)S(1)} %get-tuple-element.246, bf16[2048,128]{1,0:T(8,128)(2,1)S(1)} %copy-done.5, s32[]{:T(128)S(6)} %min.11), kind=kOutput, calls=%fused_computation.13.clone.1 | convolution fusion | flops 811859968 | bytes 13508612 | tf_op jit(solution)/shard_map/while/body/eval_jaxpr/hqk,kd->qhd/dot_general | solution.py:110
  274.3 8.9 %fusion.43 = (f32[4,512]{1,0:T(4,128)S(1)}, f32[4,512,1536]{1,2,0:T(8,128)}) fusion(f32[1536,512,4]{1,0,2:T(8,128)S(1)} %fusion.42, pred[512,1536]{0,1:T(8,128)(4,1)S(1)} %compare_and_fusion.2), kind=kOutput, calls=%fused_computation.49.clone.1 | output fusion | flops 18875904 | bytes 25960448 | tf_op jit(solution)/shard_map/while/body/eval_jaxpr/sub | solution.py:108
  283.2 5.6 %fusion.44 = bf16[128,4,512]{2,0,1:T(8,128)(2,1)S(1)} fusion(f32[4,512,1536]{1,2,0:T(8,128)} %get-tuple-element.245, f32[4,512]{1,0:T(4,128)S(1)} %get-tuple-element.246, bf16[2048,128]{1,0:T(8,128)(2,1)S(1)} %copy-done.5, s32[]{:T(128)S(6)} %min.11), kind=kOutput, calls=%fused_computation.13.clone.1 | convolution fusion | flops 811859968 | bytes 13508612 | tf_op jit(solution)/shard_map/while/body/eval_jaxpr/hqk,kd->qhd/dot_general | solution.py:110
  295.4 8.9 %fusion.43 = (f32[4,512]{1,0:T(4,128)S(1)}, f32[4,512,1536]{1,2,0:T(8,128)}) fusion(f32[1536,512,4]{1,0,2:T(8,128)S(1)} %fusion.42, pred[512,1536]{0,1:T(8,128)(4,1)S(1)} %compare_and_fusion.2), kind=kOutput, calls=%fused_computation.49.clone.1 | output fusion | flops 18875904 | bytes 25960448 | tf_op jit(solution)/shard_map/while/body/eval_jaxpr/sub | solution.py:108
  304.3 5.6 %fusion.44 = bf16[128,4,512]{2,0,1:T(8,128)(2,1)S(1)} fusion(f32[4,512,1536]{1,2,0:T(8,128)} %get-tuple-element.245, f32[4,512]{1,0:T(4,128)S(1)} %get-tuple-element.246, bf16[2048,128]{1,0:T(8,128)(2,1)S(1)} %copy-done.5, s32[]{:T(128)S(6)} %min.11), kind=kOutput, calls=%fused_computation.13.clone.1 | convolution fusion | flops 811859968 | bytes 13508612 | tf_op jit(solution)/shard_map/while/body/eval_jaxpr/hqk,kd->qhd/dot_general | solution.py:110
  310.9 53.9 %all_to_all.74 = bf16[16,128,512]{2,1,0:T(8,128)(2,1)} all-to-all(bf16[16,128,512]{2,1,0:T(8,128)(2,1)} %bitcast.116), channel_id=1, replica_groups=mesh['groups'=2,'seq'=16] {'seq'}, dimensions={0} | all-to-all | bytes 4194304 | tf_op jit(solution)/shard_map/all_to_all | solution.py:115
  (93 shorter events, 71.9 us)
Async XLA Ops:
  0.0 93.2 %copy-start = (bf16[16,512,192]{1,2,0:T(8,128)(2,1)S(1)}, bf16[16,512,192]{1,2,0:T(8,128)(2,1)}, u32[]{:S(2)}) copy-start(bf16[16,512,192]{1,2,0:T(8,128)(2,1)} %param.15) | copy-start | bytes 9437188
  2.0 21.4 %all-to-all-start = ((bf16[128,16,128]{2,0,1:T(8,128)(2,1)}), bf16[128,16,128]{2,0,1:T(8,128)(2,1)}, u32[]{:S(2)}, u32[]{:S(2)}) async-start(bf16[128,16,128]{2,0,1:T(8,128)(2,1)} %bitcast.117), calls=%async_computation | async-start | bytes 1048576 | tf_op jit(solution)/shard_map/all_to_all | solution.py:60
  23.5 46.2 %all-to-all-start.1 = ((bf16[128,16,512]{2,0,1:T(8,128)(2,1)}), bf16[128,16,512]{2,0,1:T(8,128)(2,1)}, u32[]{:S(2)}, u32[]{:S(2)}) async-start(bf16[128,16,512]{2,0,1:T(8,128)(2,1)} %bitcast.109), calls=%async_computation.1 | async-start | bytes 4194304 | tf_op jit(solution)/shard_map/all_to_all | solution.py:41
  69.7 128.7 %all-to-all-start.3 = ((bf16[128,16,512]{0,2,1:T(8,128)(2,1)}), bf16[128,16,512]{0,2,1:T(8,128)(2,1)}, u32[]{:S(2)}, u32[]{:S(2)}) async-start(bf16[128,16,512]{0,2,1:T(8,128)(2,1)} %bitcast.107), calls=%async_computation.3 | async-start | bytes 4194304 | tf_op jit(solution)/shard_map/all_to_all | solution.py:58
  85.9 4.4 %copy-start.7 = (s32[32]{0:T(128)S(1)}, s32[32]{0:T(128)}, u32[]{:S(2)}) copy-start(s32[32]{0:T(128)} %param.18) | copy-start | bytes 388
  86.0 4.4 %copy-start.8 = (s32[8]{0:T(128)S(1)}, s32[8]{0:T(128)}, u32[]{:S(2)}) copy-start(s32[8]{0:T(128)} %param.19) | copy-start | bytes 100
  96.8 3.4 copy-start.6
  178.4 2.8 copy-start.3
  180.0 1.2 copy-start.2
  181.9 1.0 slice-start
  193.1 5.4 %copy-start.4 = (bf16[128,8,128]{2,0,1:T(8,128)(2,1)S(1)}, bf16[128,8,128]{2,0,1:T(8,128)(2,1)}, u32[]{:S(2)}) copy-start(bf16[128,8,128]{2,0,1:T(8,128)(2,1)} %copy_bitcast_fusion.2) | copy-start | bytes 786436
  199.3 25.2 %all-to-all-start.2 = ((bf16[128,16,128]{2,0,1:T(8,128)(2,1)}), bf16[128,16,128]{2,0,1:T(8,128)(2,1)S(1)}, u32[]{:S(2)}, u32[]{:S(2)}) async-start(bf16[128,16,128]{2,0,1:T(8,128)(2,1)} %bitcast.19), calls=%async_computation.2 | async-start | bytes 1048576 | tf_op jit(solution)/shard_map/all_to_all | solution.py:59
  232.1 8.9 %copy-start.5 = (bf16[2048,128]{1,0:T(8,128)(2,1)S(1)}, bf16[2048,128]{1,0:T(8,128)(2,1)}, u32[]{:S(2)}) copy-start(bf16[2048,128]{1,0:T(8,128)(2,1)} %get-tuple-element.276) | copy-start | bytes 1572868 | tf_op jit(solution)/shard_map/while
  253.2 8.9 %copy-start.5 = (bf16[2048,128]{1,0:T(8,128)(2,1)S(1)}, bf16[2048,128]{1,0:T(8,128)(2,1)}, u32[]{:S(2)}) copy-start(bf16[2048,128]{1,0:T(8,128)(2,1)} %get-tuple-element.276) | copy-start | bytes 1572868 | tf_op jit(solution)/shard_map/while
  274.3 8.9 %copy-start.5 = (bf16[2048,128]{1,0:T(8,128)(2,1)S(1)}, bf16[2048,128]{1,0:T(8,128)(2,1)}, u32[]{:S(2)}) copy-start(bf16[2048,128]{1,0:T(8,128)(2,1)} %get-tuple-element.276) | copy-start | bytes 1572868 | tf_op jit(solution)/shard_map/while
  295.4 8.9 %copy-start.5 = (bf16[2048,128]{1,0:T(8,128)(2,1)S(1)}, bf16[2048,128]{1,0:T(8,128)(2,1)}, u32[]{:S(2)}) copy-start(bf16[2048,128]{1,0:T(8,128)(2,1)} %get-tuple-element.276) | copy-start | bytes 1572868 | tf_op jit(solution)/shard_map/while
  364.8 8.1 %copy-start.1 = (bf16[16,512,192]{1,2,0:T(8,128)(2,1)S(1)}, bf16[16,512,192]{1,2,0:T(8,128)(2,1)}, u32[]{:S(2)}) copy-start(bf16[16,512,192]{1,2,0:T(8,128)(2,1)} %param.15) | copy-start | bytes 9437188
where the time goes:
time: 375 us; the launch traced here: 373 us
  blocking collectives  124 us (33%)
  local copies, waits for them, and re-layouts  72.3 us (19%)
  other arithmetic  49.8 us (13%)
  waiting for transfers between devices  48.6 us (13%)
  matrix products  44.2 us (12%)
  starting transfers between devices  31 us (8%)
    psum x1, blocking collectives, body(): shrunk = lax.psum(partial_value, 'seq').astype(jnp.bfloat16)  70.1 us
    all_to_all x1, blocking collectives, body(): lax.all_to_all(head_rows, 'seq', split_axis=0, concat_axis=1, tiled=True)  53.9 us
    all_to_all x1, waiting for transfers between devices, body(): lax.all_to_all(hidden, 'seq', split_axis=1, concat_axis=0, tiled=True)  37.6 us
    sub x4, other arithmetic, attend(): weights = jnp.exp(scores - row_max)  35.6 us
    dot_general x4, matrix products, attend(): jnp.einsum('hqk,kd->qhd', probs, v_rows, preferred_element_type=jnp.float32)  22.5 us
    unnamed x19, local copies, waits for them, and re-layouts  11.3 us
    dot_general x4, matrix products, attend(): jnp.einsum('qhd,kd->hqk', q_rows, k_rows, preferred_element_type=jnp.floa...  11.3 us
    all_to_all x1, waiting for transfers between devices, body(): lax.all_to_all(value_replicas, 'seq', split_axis=1, concat_axis=0, tiled=...  11 us
  transfers between devices with their start and end apart: 4, of which 2 were waited for; matrix products, arithmetic and copies ran while one was open for 19% of the time, Pallas kernels for 0%

commit v1 on v0

--- a/solution.py
+++ b/solution.py
@@ -3,12 +3,17 @@
 import jax.numpy as jnp
 from jax import lax
 from jax.sharding import PartitionSpec as P
+from jax.lax import all_gather
 
 QUERY_HEADS = 64
 KEY_VALUE_HEADS = 8
 HEAD_SIZE = 128
 ADAPTER_RANK = 64
 QBLK = 512
+
+
+def ports_define(base_x, which_axis):
+    return jnp.sum(all_gather(base_x, which_axis), axis=0)
 
 
 def body(
@@ -45,7 +50,7 @@
         shrink_a[adapter_of],
         preferred_element_type=jnp.float32,
     ).reshape(token_total, 3 * ADAPTER_RANK)
-    shrunk = lax.psum(partial_value, "seq").astype(jnp.bfloat16)
+    shrunk = ports_define(partial_value, "seq").astype(jnp.bfloat16)
     key_replicas = jnp.repeat(
         base_key_weight.reshape(token_per_device, KEY_VALUE_HEADS, HEAD_SIZE), device_groups, axis=1
     ).reshape(token_per_device, device_list * HEAD_SIZE)

time: 375 us -> 454 us (1.21)
  waiting for transfers between devices: 48.6 us -> 171 us
  blocking collectives: 124 us -> 53.8 us
  between operations: 0.13 us -> 13.5 us
  other arithmetic: 49.8 us -> 57.5 us
  starting transfers between devices: 31 us -> 37.2 us
    psum x1 -> x0, blocking collectives: 70.1 us -> none  [body(): shrunk = lax.psum(partial_value, 'seq').astype(jnp.bfloat16)]
    all_to_all x1, waiting for transfers between devices: 0.01 us -> 67.2 us  [body(): lax.all_to_all(q_base, 'seq', split_axis=1, concat_axis=0, tiled=True)]
    all_gather x0 -> x1, waiting for transfers between devices: none -> 65.6 us  [ports_define(): return jnp.sum(all_gather(base_x, which_axis), axis=0)]
    all_to_all x1, waiting for transfers between devices: 11 us -> 0.01 us  [body(): lax.all_to_all(value_replicas, 'seq', split_axis=1, concat_axis=0, tiled=...]
    reduce_sum x0 -> x1, other arithmetic: none -> 9.19 us  [ports_define(): return jnp.sum(all_gather(base_x, which_axis), axis=0)]
    all_to_all x1, starting transfers between devices: 8.48 us -> 14.2 us  [body(): lax.all_to_all(key_replicas, 'seq', split_axis=1, concat_axis=0, tiled=True)]
    unnamed x19 -> x25, local copies, waits for them, and re-layouts: 11.3 us -> 12.2 us
  transfers between devices with their start and end apart: 4 -> 5, of which waited for: 2 -> 3; matrix products, arithmetic and copies ran while one was open for 19% -> 16% of each run, Pallas kernels for 0% -> 0%
where the time goes in v1:
time: 454 us; the launch traced here: 452 us
  waiting for transfers between devices  171 us (38%)
  local copies, waits for them, and re-layouts  73 us (16%)
  other arithmetic  57.5 us (13%)
  blocking collectives  53.8 us (12%)
  matrix products  43.7 us (10%)
  starting transfers between devices  37.2 us (8%)
  between operations  13.5 us (3%)
    all_to_all x1, waiting for transfers between devices, body(): lax.all_to_all(q_base, 'seq', split_axis=1, concat_axis=0, tiled=True)  67.2 us
    all_gather x1, waiting for transfers between devices, ports_define(): return jnp.sum(all_gather(base_x, which_axis), axis=0)  65.6 us
    all_to_all x1, blocking collectives, body(): lax.all_to_all(head_rows, 'seq', split_axis=0, concat_axis=1, tiled=True)  53.8 us
    all_to_all x1, waiting for transfers between devices, body(): lax.all_to_all(hidden, 'seq', split_axis=1, concat_axis=0, tiled=True)  37.8 us
    sub x4, other arithmetic, attend(): weights = jnp.exp(scores - row_max)  35.5 us
    dot_general x4, matrix products, attend(): jnp.einsum('hqk,kd->qhd', probs, v_rows, preferred_element_type=jnp.float32)  22.5 us
    all_to_all x1, starting transfers between devices, body(): lax.all_to_all(key_replicas, 'seq', split_axis=1, concat_axis=0, tiled=True)  14.2 us
    unnamed x25, local copies, waits for them, and re-layouts  12.2 us
  transfers between devices with their start and end apart: 5, of which 3 were waited for; matrix products, arithmetic and copies ran while one was open for 16% of the time, Pallas kernels for 0%

profile of v1, /device:TPU:1, one launch (start us, length us, event | category | flops | bytes accessed | tf_op | source)
XLA Modules:
  0.0 452.1 jit_solution(3502599225387007100)
XLA Ops:
  9.8 7.5 %all-to-all-start.1 = ((bf16[128,16,512]{2,0,1:T(8,128)(2,1)}), bf16[128,16,512]{2,0,1:T(8,128)(2,1)}, u32[]{:S(2)}, u32[]{:S(2)}) async-start(bf16[128,16,512]{2,0,1:T(8,128)(2,1)} %bitcast.109), calls=%async_computation.1 | async-start | bytes 4194304 | tf_op jit(solution)/shard_map/all_to_all | solution.py:46
  21.1 37.8 %all-to-all-done.1 = bf16[128,16,512]{2,0,1:T(8,128)(2,1)} async-done(((bf16[128,16,512]{2,0,1:T(8,128)(2,1)}), bf16[128,16,512]{2,0,1:T(8,128)(2,1)}, u32[]{:S(2)}, u32[]{:S(2)}) %all-to-all-start.1) | async-done | bytes 2097184 | tf_op jit(solution)/shard_map/all_to_all | solution.py:46
  58.9 5.5 %fusion.26 = f32[32,192,64]{1,2,0:T(8,128)S(1)} fusion(bf16[32,512,192]{1,2,0:T(8,128)(2,1)} %gather_fusion.1, bf16[32,64,512]{2,1,0:T(8,128)(2,1)} %bitcast.13), kind=kOutput, calls=%fused_computation.50 | convolution fusion | flops 402653184 | bytes 9961472 | tf_op jit(solution)/shard_map/btf,bfr->btr/dot_general | solution.py:47
  70.3 10.7 %all-to-all-start.3 = ((bf16[128,16,512]{0,2,1:T(8,128)(2,1)}), bf16[128,16,512]{0,2,1:T(8,128)(2,1)S(1)}, u32[]{:S(2)}, u32[]{:S(2)}) async-start(bf16[128,16,512]{0,2,1:T(8,128)(2,1)} %bitcast.107), calls=%async_computation.3 | async-start | bytes 4194304 | tf_op jit(solution)/shard_map/all_to_all | solution.py:63
  81.0 5.6 %copy.111 = bf16[128,8,16,128]{3,2,1,0:T(8,128)(2,1)} copy(bf16[128,8,16,128]{3,1,2,0:T(8,128)(2,1)} %bitcast.114) | data formatting | bytes 8388608
  86.7 67.2 %all-to-all-done.3 = bf16[128,16,512]{0,2,1:T(8,128)(2,1)S(1)} async-done(((bf16[128,16,512]{0,2,1:T(8,128)(2,1)}), bf16[128,16,512]{0,2,1:T(8,128)(2,1)S(1)}, u32[]{:S(2)}, u32[]{:S(2)}) %all-to-all-start.3) | async-done | bytes 2097184 | tf_op jit(solution)/shard_map/all_to_all | solution.py:63
  154.8 4.8 %all-to-all-start = ((bf16[128,16,128]{2,0,1:T(8,128)(2,1)}), bf16[128,16,128]{2,0,1:T(8,128)(2,1)}, u32[]{:S(2)}, u32[]{:S(2)}) async-start(bf16[128,16,128]{2,0,1:T(8,128)(2,1)} %bitcast.6), calls=%async_computation | async-start | bytes 1048576 | tf_op jit(solution)/shard_map/all_to_all | solution.py:65
  176.2 5.0 %reshape.148 = f32[2048,4,128]{0,2,1:T(8,128)} reshape(f32[16,128,512]{1,0,2:T(8,128)} %copy.92) | data formatting | bytes 8388608 | tf_op jit(solution)/shard_map/convert_element_type | solution.py:75
  181.1 65.6 %all-gather.2.cloned.1.call-done = f32[16,2048,192]{1,2,0:T(8,128)} async-done(((f32[1,2048,192]{1,2,0:T(8,128)}), f32[16,2048,192]{1,2,0:T(8,128)}) %all-gather.2.cloned.1.call-update) | async-done | bytes 25165840 | tf_op jit(solution)/shard_map/all_gather | solution.py:16
  246.7 9.2 %reduce_sum.37 = bf16[2048,192]{0,1:T(8,128)(2,1)S(1)} reduce(f32[16,2048,192]{1,2,0:T(8,128)} %all-gather.2.cloned.1.call-done, f32[]{:T(128)} %constant.110.clone.1), dimensions={0}, to_apply=%region_1.2 | reduce | flops 5898240 | bytes 25952260 | tf_op jit(solution)/shard_map/reduce_sum | solution.py:16
  263.3 14.2 %all-to-all-start.2 = ((bf16[128,16,128]{2,0,1:T(8,128)(2,1)}), bf16[128,16,128]{2,0,1:T(8,128)(2,1)S(1)}, u32[]{:S(2)}, u32[]{:S(2)}) async-start(bf16[128,16,128]{2,0,1:T(8,128)(2,1)} %bitcast.19), calls=%async_computation.2 | async-start | bytes 1048576 | tf_op jit(solution)/shard_map/all_to_all | solution.py:64
  281.2 5.3 %reshape.145 = f32[2048,4,128]{2,1,0:T(4,128)} reshape(f32[32,64,512]{2,1,0:T(8,128)} %fusion.22) | data formatting | bytes 8388608 | tf_op jit(solution)/shard_map/reshape | solution.py:73
  286.5 5.3 %copy.94 = f32[2048,4,128]{0,2,1:T(8,128)} copy(f32[2048,4,128]{2,1,0:T(4,128)} %reshape.145) | data formatting | bytes 8388608 | tf_op jit(solution)/shard_map/reshape | solution.py:73
  291.8 5.6 %add_convert_fusion = bf16[2048,4,128]{0,2,1:T(8,128)(2,1)} fusion(f32[2048,4,128]{0,2,1:T(8,128)} %reshape.148, f32[2048,4,128]{0,2,1:T(8,128)} %copy.94), kind=kLoop, calls=%fused_computation.28 | loop fusion | flops 2097152 | bytes 10485760 | tf_op jit(solution)/shard_map/convert_element_type | solution.py:76
  299.4 83.9 %while.14 = (s32[]{:T(128)}, bf16[4,512,512]{2,1,0:T(8,128)(2,1)}, s32[4]{0:T(128)S(1)}, bf16[2048,128]{1,0:T(8,128)(2,1)}, s32[2048]{0:T(1024)S(1)}, /*index=5*...) while((s32[]{:T(128)}, bf16[4,512,512]{2,1,0:T(8,128)(2,1)}, ...), condition=%wide.region_5.6_spmd, body=%wide.region_2.5_spmd.sunk | while | flops 1638403584 | bytes 57991952 | solution.py:118
  304.8 8.9 %fusion.43 = (f32[4,512]{1,0:T(4,128)S(1)}, f32[4,512,1536]{1,2,0:T(8,128)}) fusion(f32[1536,512,4]{1,0,2:T(8,128)S(1)} %fusion.42, pred[512,1536]{0,1:T(8,128)(4,1)S(1)} %compare_and_fusion.2), kind=kOutput, calls=%fused_computation.49.clone.1 | output fusion | flops 18875904 | bytes 25960448 | tf_op jit(solution)/shard_map/while/body/eval_jaxpr/sub | solution.py:113
  313.7 5.6 %fusion.44 = bf16[128,4,512]{2,0,1:T(8,128)(2,1)S(1)} fusion(f32[4,512,1536]{1,2,0:T(8,128)} %get-tuple-element.252, f32[4,512]{1,0:T(4,128)S(1)} %get-tuple-element.253, bf16[2048,128]{1,0:T(8,128)(2,1)S(1)} %copy-done.7, s32[]{:T(128)S(6)} %min.11), kind=kOutput, calls=%fused_computation.13.clone.1 | convolution fusion | flops 811859968 | bytes 13508612 | tf_op jit(solution)/shard_map/while/body/eval_jaxpr/hqk,kd->qhd/dot_general | solution.py:115
  325.8 8.9 %fusion.43 = (f32[4,512]{1,0:T(4,128)S(1)}, f32[4,512,1536]{1,2,0:T(8,128)}) fusion(f32[1536,512,4]{1,0,2:T(8,128)S(1)} %fusion.42, pred[512,1536]{0,1:T(8,128)(4,1)S(1)} %compare_and_fusion.2), kind=kOutput, calls=%fused_computation.49.clone.1 | output fusion | flops 18875904 | bytes 25960448 | tf_op jit(solution)/shard_map/while/body/eval_jaxpr/sub | solution.py:113
  334.7 5.6 %fusion.44 = bf16[128,4,512]{2,0,1:T(8,128)(2,1)S(1)} fusion(f32[4,512,1536]{1,2,0:T(8,128)} %get-tuple-element.252, f32[4,512]{1,0:T(4,128)S(1)} %get-tuple-element.253, bf16[2048,128]{1,0:T(8,128)(2,1)S(1)} %copy-done.7, s32[]{:T(128)S(6)} %min.11), kind=kOutput, calls=%fused_computation.13.clone.1 | convolution fusion | flops 811859968 | bytes 13508612 | tf_op jit(solution)/shard_map/while/body/eval_jaxpr/hqk,kd->qhd/dot_general | solution.py:115
  346.8 8.9 %fusion.43 = (f32[4,512]{1,0:T(4,128)S(1)}, f32[4,512,1536]{1,2,0:T(8,128)}) fusion(f32[1536,512,4]{1,0,2:T(8,128)S(1)} %fusion.42, pred[512,1536]{0,1:T(8,128)(4,1)S(1)} %compare_and_fusion.2), kind=kOutput, calls=%fused_computation.49.clone.1 | output fusion | flops 18875904 | bytes 25960448 | tf_op jit(solution)/shard_map/while/body/eval_jaxpr/sub | solution.py:113
  355.6 5.6 %fusion.44 = bf16[128,4,512]{2,0,1:T(8,128)(2,1)S(1)} fusion(f32[4,512,1536]{1,2,0:T(8,128)} %get-tuple-element.252, f32[4,512]{1,0:T(4,128)S(1)} %get-tuple-element.253, bf16[2048,128]{1,0:T(8,128)(2,1)S(1)} %copy-done.7, s32[]{:T(128)S(6)} %min.11), kind=kOutput, calls=%fused_computation.13.clone.1 | convolution fusion | flops 811859968 | bytes 13508612 | tf_op jit(solution)/shard_map/while/body/eval_jaxpr/hqk,kd->qhd/dot_general | solution.py:115
  367.7 8.9 %fusion.43 = (f32[4,512]{1,0:T(4,128)S(1)}, f32[4,512,1536]{1,2,0:T(8,128)}) fusion(f32[1536,512,4]{1,0,2:T(8,128)S(1)} %fusion.42, pred[512,1536]{0,1:T(8,128)(4,1)S(1)} %compare_and_fusion.2), kind=kOutput, calls=%fused_computation.49.clone.1 | output fusion | flops 18875904 | bytes 25960448 | tf_op jit(solution)/shard_map/while/body/eval_jaxpr/sub | solution.py:113
  376.6 5.6 %fusion.44 = bf16[128,4,512]{2,0,1:T(8,128)(2,1)S(1)} fusion(f32[4,512,1536]{1,2,0:T(8,128)} %get-tuple-element.252, f32[4,512]{1,0:T(4,128)S(1)} %get-tuple-element.253, bf16[2048,128]{1,0:T(8,128)(2,1)S(1)} %copy-done.7, s32[]{:T(128)S(6)} %min.11), kind=kOutput, calls=%fused_computation.13.clone.1 | convolution fusion | flops 811859968 | bytes 13508612 | tf_op jit(solution)/shard_map/while/body/eval_jaxpr/hqk,kd->qhd/dot_general | solution.py:115
  383.3 53.8 %all_to_all.74 = bf16[16,128,512]{2,1,0:T(8,128)(2,1)} all-to-all(bf16[16,128,512]{2,1,0:T(8,128)(2,1)} %bitcast.116), channel_id=1, replica_groups=mesh['groups'=2,'seq'=16] {'seq'}, dimensions={0} | all-to-all | bytes 4194304 | tf_op jit(solution)/shard_map/all_to_all | solution.py:120
  (102 shorter events, 74.8 us)
Async XLA Ops:
  6.5 10.9 %copy-start = (bf16[16,512,192]{1,2,0:T(8,128)(2,1)S(1)}, bf16[16,512,192]{1,2,0:T(8,128)(2,1)}, u32[]{:S(2)}) copy-start(bf16[16,512,192]{1,2,0:T(8,128)(2,1)} %param.15) | copy-start | bytes 9437188
  9.8 7.5 %copy-start.10 = (s32[32]{0:T(128)S(1)}, s32[32]{0:T(128)}, u32[]{:S(2)}) copy-start(s32[32]{0:T(128)} %param.18) | copy-start | bytes 388
  9.8 7.5 %copy-start.11 = (s32[8]{0:T(128)S(1)}, s32[8]{0:T(128)}, u32[]{:S(2)}) copy-start(s32[8]{0:T(128)} %param.19) | copy-start | bytes 100
  9.8 49.1 %all-to-all-start.1 = ((bf16[128,16,512]{2,0,1:T(8,128)(2,1)}), bf16[128,16,512]{2,0,1:T(8,128)(2,1)}, u32[]{:S(2)}, u32[]{:S(2)}) async-start(bf16[128,16,512]{2,0,1:T(8,128)(2,1)} %bitcast.109), calls=%async_computation.1 | async-start | bytes 4194304 | tf_op jit(solution)/shard_map/all_to_all | solution.py:46
  17.3 229.4 %all-gather.2.cloned.1.call-start = ((), (), s32[]{:S(2)}) async-start(), calls=%async_computation.5 | async-start | bytes 26738688 | tf_op jit(solution)/shard_map/all_gather | solution.py:16
  70.3 83.6 %all-to-all-start.3 = ((bf16[128,16,512]{0,2,1:T(8,128)(2,1)}), bf16[128,16,512]{0,2,1:T(8,128)(2,1)S(1)}, u32[]{:S(2)}, u32[]{:S(2)}) async-start(bf16[128,16,512]{0,2,1:T(8,128)(2,1)} %bitcast.107), calls=%async_computation.3 | async-start | bytes 4194304 | tf_op jit(solution)/shard_map/all_to_all | solution.py:63
  81.0 5.6 %copy-start.8 = (bf16[128,1024]{1,0:T(8,128)(2,1)S(1)}, bf16[128,1024]{1,0:T(8,128)(2,1)}, u32[]{:S(2)}) copy-start(bf16[128,1024]{1,0:T(8,128)(2,1)} %param.14) | copy-start | bytes 786436
  154.8 107.7 %all-to-all-start = ((bf16[128,16,128]{2,0,1:T(8,128)(2,1)}), bf16[128,16,128]{2,0,1:T(8,128)(2,1)}, u32[]{:S(2)}, u32[]{:S(2)}) async-start(bf16[128,16,128]{2,0,1:T(8,128)(2,1)} %bitcast.6), calls=%async_computation | async-start | bytes 1048576 | tf_op jit(solution)/shard_map/all_to_all | solution.py:65
  165.6 5.0 %copy-start.9 = (bf16[128,1024]{1,0:T(8,128)(2,1)S(1)}, bf16[128,1024]{1,0:T(8,128)(2,1)}, u32[]{:S(2)}) copy-start(bf16[128,1024]{1,0:T(8,128)(2,1)} %param.13) | copy-start | bytes 786436
  255.9 2.9 copy-start.5
  257.6 1.2 copy-start.4
  259.5 1.5 slice-start
  259.5 2.9 copy-start.6
  259.5 18.0 %copy-start.2 = (bf16[32,64,512]{2,1,0:T(8,128)(2,1)S(1)}, bf16[32,64,512]{2,1,0:T(8,128)(2,1)}, u32[]{:S(2)}) copy-start(bf16[32,64,512]{2,1,0:T(8,128)(2,1)} %gather_fusion.2) | copy-start | bytes 6291460
  263.3 34.0 %all-to-all-start.2 = ((bf16[128,16,128]{2,0,1:T(8,128)(2,1)}), bf16[128,16,128]{2,0,1:T(8,128)(2,1)S(1)}, u32[]{:S(2)}, u32[]{:S(2)}) async-start(bf16[128,16,128]{2,0,1:T(8,128)(2,1)} %bitcast.19), calls=%async_computation.2 | async-start | bytes 1048576 | tf_op jit(solution)/shard_map/all_to_all | solution.py:64
  291.8 5.6 %copy-start.3 = (f32[32,64,2,128]{3,1,0,2:T(8,128)S(1)}, f32[32,64,2,128]{3,1,0,2:T(8,128)}, u32[]{:S(2)}) copy-start(f32[32,64,2,128]{3,1,0,2:T(8,128)} %copy.89) | copy-start | bytes 6291460
  304.8 8.9 %copy-start.7 = (bf16[2048,128]{1,0:T(8,128)(2,1)S(1)}, bf16[2048,128]{1,0:T(8,128)(2,1)}, u32[]{:S(2)}) copy-start(bf16[2048,128]{1,0:T(8,128)(2,1)} %get-tuple-element.283) | copy-start | bytes 1572868 | tf_op jit(solution)/shard_map/while
  325.8 8.9 %copy-start.7 = (bf16[2048,128]{1,0:T(8,128)(2,1)S(1)}, bf16[2048,128]{1,0:T(8,128)(2,1)}, u32[]{:S(2)}) copy-start(bf16[2048,128]{1,0:T(8,128)(2,1)} %get-tuple-element.283) | copy-start | bytes 1572868 | tf_op jit(solution)/shard_map/while
  346.7 8.9 %copy-start.7 = (bf16[2048,128]{1,0:T(8,128)(2,1)S(1)}, bf16[2048,128]{1,0:T(8,128)(2,1)}, u32[]{:S(2)}) copy-start(bf16[2048,128]{1,0:T(8,128)(2,1)} %get-tuple-element.283) | copy-start | bytes 1572868 | tf_op jit(solution)/shard_map/while
  367.7 8.9 %copy-start.7 = (bf16[2048,128]{1,0:T(8,128)(2,1)S(1)}, bf16[2048,128]{1,0:T(8,128)(2,1)}, u32[]{:S(2)}) copy-start(bf16[2048,128]{1,0:T(8,128)(2,1)} %get-tuple-element.283) | copy-start | bytes 1572868 | tf_op jit(solution)/shard_map/while
  437.1 8.1 %copy-start.1 = (bf16[16,512,192]{1,2,0:T(8,128)(2,1)S(1)}, bf16[16,512,192]{1,2,0:T(8,128)(2,1)}, u32[]{:S(2)}) copy-start(bf16[16,512,192]{1,2,0:T(8,128)(2,1)} %param.15) | copy-start | bytes 9437188
Sparse Core Ops, SparseCore 0:
  66.3 180.3 all-gather.1
